TPU v7x, 32 devices: a whole 2x2x4 slice. The times are simulated.
32 devices in a mesh: rows: 8 (over z, y), dims: 4 (over x, core).
Axes of the slice: x: 2, y: 2, z: 4, core: 2. Of those that a mesh axis runs over, the one named last changes fastest.
Arguments:
- table: bfloat16 [1, 256, 32768], P(None, 'dims', 'rows'), may hold values from -6 to 6
- accum: float32 [1, 32768], P(None, 'rows'), may hold values from 0.5 to 8
- grad_pooled: bfloat16 [1, 256, 1024], P(None, 'dims', 'rows'), may hold values from -6 to 6
- sample_slot: int32 [1, 8, 8, 1280], P(None, 'rows'), may hold values from 0 to 127
- row_slot: int32 [1, 8, 8, 1280], P(None, 'rows'), may hold values from 0 to 4095
- weight: int32 [1, 8, 8, 1280], P(None, 'rows'), may hold values from 1 to 3
- send_count: int32 [1, 8, 8], P(None, 'rows'), may hold values from 1 to 1280, as said below
Outputs:
- pooled: float32 [1, 256, 1024], P(None, 'dims', 'rows')
- new_table: bfloat16 [1, 256, 32768], P(None, 'dims', 'rows')
- new_accum: float32 [1, 32768], P(None, 'rows')
Inputs may be any that keep to these rules, and one draw needn't show every extreme that they name: `send_count`: at most 1280 live entries from one row shard to one owner per feature; in every feature one owner receives exactly 1280 from every row shard. Slots at or after the count are unused.
All inputs are finite; a program needn't handle non-finite values.
Results may differ from a plain program's by a relative error of at most 0.001.
Values may be sent and summed in bfloat16 or wider, within the bound.
No kernel may reach another device: no remote copies, remote signals or barrier semaphores. Data moves between devices by JAX's collectives and lax.ppermute only.
A program may use at most 64 MiB of HBM per device.

v0:
```python
import math
import jax
import jax.numpy as jnp
from jax import lax
from jax.sharding import PartitionSpec as P

D = 256
step_size = 0.3


def shards(table, accum, grad_pooled, sample_slot, row_slot, weight, send_count):
    feat_count, dim_local, row_local = table.shape
    peer_count = lax.axis_size("rows")
    own_samples = grad_pooled.shape[2]
    slot_count = sample_slot.shape[3]
    entry_count = peer_count * slot_count
    block_rows = math.gcd(row_local, 512)
    block_count = row_local // block_rows
    sample_local = sample_slot.reshape(feat_count, peer_count, slot_count)
    row_index = row_slot.reshape(feat_count, peer_count, slot_count)
    flat_rows = row_index.reshape(feat_count, 1, entry_count)
    live_count = send_count.reshape(feat_count, peer_count)
    slot_iota = lax.broadcasted_iota(jnp.int32, (1, 1, slot_count), 2)
    live_mask = slot_iota < live_count[:, :, None]
    weights = jnp.where(live_mask, weight.reshape(feat_count, peer_count, slot_count), 0)
    flat_weights = weights.reshape(feat_count, 1, entry_count).astype(jnp.bfloat16)
    block_iota = lax.broadcasted_iota(jnp.int32, (1, block_rows, 1), 1)

    def lookup_block(carry, block):
        start = block * block_rows
        table_part = lax.dynamic_slice_in_dim(table, start, block_rows, 2)
        selector = (flat_rows == block_iota + start).astype(jnp.bfloat16)
        return (
            carry
            + jnp.einsum("fdr,fre->fde", table_part, selector, preferred_element_type=jnp.float32),
            None,
        )

    looked_up, _ = lax.scan(
        lookup_block,
        jnp.zeros((feat_count, dim_local, entry_count), jnp.float32),
        jnp.arange(block_count, dtype=jnp.int32),
    )
    picked = looked_up.astype(jnp.bfloat16).reshape(feat_count, dim_local, peer_count, slot_count)
    positions = lax.broadcasted_iota(jnp.int32, (1, 1, 1, own_samples), 3)
    onehot = jnp.where(sample_local[..., None] == positions, weights[..., None], 0).astype(
        jnp.bfloat16
    )
    pooled = lax.psum_scatter(
        jnp.einsum("fdnk,fnkj->nfdj", picked, onehot, preferred_element_type=jnp.float32),
        "rows",
        scatter_dimension=0,
        tiled=True,
    ).reshape(feat_count, dim_local, own_samples)
    all_grads = lax.all_gather(grad_pooled, "rows", axis=2, tiled=True)
    all_grads = all_grads.reshape(feat_count, dim_local, peer_count, own_samples)
    selector = (sample_local[..., None] == positions).astype(jnp.bfloat16)
    entry_values = jnp.einsum(
        "fdnj,fnkj->fdnk", all_grads, selector, preferred_element_type=jnp.float32
    ).astype(jnp.bfloat16)
    entry_flat = entry_values.reshape(feat_count, dim_local, entry_count)

    def gradient_block(block):
        start = block * block_rows
        weighted = jnp.where(flat_rows == block_iota + start, flat_weights, 0)
        return jnp.einsum("fde,fre->fdr", entry_flat, weighted, preferred_element_type=jnp.float32)

    grad_blocks = lax.map(gradient_block, jnp.arange(block_count, dtype=jnp.int32))
    row_grad = jnp.moveaxis(grad_blocks, 0, 2).reshape(feat_count, dim_local, row_local)
    squares = jnp.sum(row_grad * row_grad, axis=1)
    norm_total = lax.psum(squares, "dims")
    new_accum = accum + norm_total / D
    new_table = (
        table.astype(jnp.float32) - step_size * row_grad / jnp.sqrt(new_accum)[:, None, :]
    ).astype(jnp.bfloat16)
    return (pooled, new_table, new_accum)


def solution(mesh):
    return jax.shard_map(
        shards,
        mesh=mesh,
        in_specs=(
            P(None, "dims", "rows"),
            P(None, "rows"),
            P(None, "dims", "rows"),
            P(None, "rows", None, None),
            P(None, "rows", None, None),
            P(None, "rows", None, None),
            P(None, "rows", None),
        ),
        out_specs=(P(None, "dims", "rows"), P(None, "dims", "rows"), P(None, "rows")),
        check_vma=False,
    )
```

profile of v0, /device:TPU:0, one launch (start us, length us, event | category | flops | bytes accessed | tf_op | source)
XLA Modules:
  0.0 151.7 jit_solution(12816893557992294160)
XLA Ops:
  7.2 0.8 reshape_reshape.3
  8.1 48.6 %while.25 = (s32[]{:T(128)}, f32[1,64,10240]{2,1,0:T(8,128)S(1)}, s32[8]{0:T(128)S(1)}, bf16[1,64,4096]{2,1,0:T(8,128)(2,1)}, s32[1,1,10240]{2,1,0:T(1,128)S(1)}...) while((s32[]{:T(128)}, f32[1,64,10240]{2,1,0:T(8,128)S(1)}, s32[8]{0:T(128)S(1)}, ...), condition=%wide.region_1.2_spmd.clone, body=%wide.region_0.1_spmd.clone.sunk | while | flops 677642752 | bytes 5353649 | solution.py:39
  8.1 0.6 dynamic_slice.25
  9.3 4.8 %fusion.55 = f32[1,64,10240]{2,1,0:T(8,128)S(1)} fusion(s32[10240]{0:T(1024)S(1)} %bitcast.90, s32[512]{0:T(512)S(1)} %bitcast.88, f32[1,64,10240]{2,1,0:T(8,128)S(1)} %get-tuple-element.264, pred[]{:T(512)S(6)} %compare.3, bf16[1,64,4096]{2,1,0:T(8,128)(2,1)} %get-tuple-element.275, s32[]{:T(128)S(6)} %select_n.63), kind=kOutput, calls=%fused_computation.5.clone.1 | convolution fusion | flops 677642240 | bytes 5351429 | tf_op jit(solution)/shard_map/while/body/eval_jaxpr/fdr,fre->fde/dot_general | solution.py:35
  14.1 0.6 dynamic_slice.25
  15.4 4.8 %fusion.55 = f32[1,64,10240]{2,1,0:T(8,128)S(1)} fusion(s32[10240]{0:T(1024)S(1)} %bitcast.90, s32[512]{0:T(512)S(1)} %bitcast.88, f32[1,64,10240]{2,1,0:T(8,128)S(1)} %get-tuple-element.264, pred[]{:T(512)S(6)} %compare.3, bf16[1,64,4096]{2,1,0:T(8,128)(2,1)} %get-tuple-element.275, s32[]{:T(128)S(6)} %select_n.63), kind=kOutput, calls=%fused_computation.5.clone.1 | convolution fusion | flops 677642240 | bytes 5351429 | tf_op jit(solution)/shard_map/while/body/eval_jaxpr/fdr,fre->fde/dot_general | solution.py:35
  20.2 0.6 dynamic_slice.25
  21.5 4.8 %fusion.55 = f32[1,64,10240]{2,1,0:T(8,128)S(1)} fusion(s32[10240]{0:T(1024)S(1)} %bitcast.90, s32[512]{0:T(512)S(1)} %bitcast.88, f32[1,64,10240]{2,1,0:T(8,128)S(1)} %get-tuple-element.264, pred[]{:T(512)S(6)} %compare.3, bf16[1,64,4096]{2,1,0:T(8,128)(2,1)} %get-tuple-element.275, s32[]{:T(128)S(6)} %select_n.63), kind=kOutput, calls=%fused_computation.5.clone.1 | convolution fusion | flops 677642240 | bytes 5351429 | tf_op jit(solution)/shard_map/while/body/eval_jaxpr/fdr,fre->fde/dot_general | solution.py:35
  26.3 0.6 dynamic_slice.25
  27.5 4.8 %fusion.55 = f32[1,64,10240]{2,1,0:T(8,128)S(1)} fusion(s32[10240]{0:T(1024)S(1)} %bitcast.90, s32[512]{0:T(512)S(1)} %bitcast.88, f32[1,64,10240]{2,1,0:T(8,128)S(1)} %get-tuple-element.264, pred[]{:T(512)S(6)} %compare.3, bf16[1,64,4096]{2,1,0:T(8,128)(2,1)} %get-tuple-element.275, s32[]{:T(128)S(6)} %select_n.63), kind=kOutput, calls=%fused_computation.5.clone.1 | convolution fusion | flops 677642240 | bytes 5351429 | tf_op jit(solution)/shard_map/while/body/eval_jaxpr/fdr,fre->fde/dot_general | solution.py:35
  32.4 0.6 dynamic_slice.25
  33.6 4.8 %fusion.55 = f32[1,64,10240]{2,1,0:T(8,128)S(1)} fusion(s32[10240]{0:T(1024)S(1)} %bitcast.90, s32[512]{0:T(512)S(1)} %bitcast.88, f32[1,64,10240]{2,1,0:T(8,128)S(1)} %get-tuple-element.264, pred[]{:T(512)S(6)} %compare.3, bf16[1,64,4096]{2,1,0:T(8,128)(2,1)} %get-tuple-element.275, s32[]{:T(128)S(6)} %select_n.63), kind=kOutput, calls=%fused_computation.5.clone.1 | convolution fusion | flops 677642240 | bytes 5351429 | tf_op jit(solution)/shard_map/while/body/eval_jaxpr/fdr,fre->fde/dot_general | solution.py:35
  38.4 0.6 dynamic_slice.25
  39.7 4.8 %fusion.55 = f32[1,64,10240]{2,1,0:T(8,128)S(1)} fusion(s32[10240]{0:T(1024)S(1)} %bitcast.90, s32[512]{0:T(512)S(1)} %bitcast.88, f32[1,64,10240]{2,1,0:T(8,128)S(1)} %get-tuple-element.264, pred[]{:T(512)S(6)} %compare.3, bf16[1,64,4096]{2,1,0:T(8,128)(2,1)} %get-tuple-element.275, s32[]{:T(128)S(6)} %select_n.63), kind=kOutput, calls=%fused_computation.5.clone.1 | convolution fusion | flops 677642240 | bytes 5351429 | tf_op jit(solution)/shard_map/while/body/eval_jaxpr/fdr,fre->fde/dot_general | solution.py:35
  44.5 0.6 dynamic_slice.25
  45.8 4.8 %fusion.55 = f32[1,64,10240]{2,1,0:T(8,128)S(1)} fusion(s32[10240]{0:T(1024)S(1)} %bitcast.90, s32[512]{0:T(512)S(1)} %bitcast.88, f32[1,64,10240]{2,1,0:T(8,128)S(1)} %get-tuple-element.264, pred[]{:T(512)S(6)} %compare.3, bf16[1,64,4096]{2,1,0:T(8,128)(2,1)} %get-tuple-element.275, s32[]{:T(128)S(6)} %select_n.63), kind=kOutput, calls=%fused_computation.5.clone.1 | convolution fusion | flops 677642240 | bytes 5351429 | tf_op jit(solution)/shard_map/while/body/eval_jaxpr/fdr,fre->fde/dot_general | solution.py:35
  50.6 0.6 dynamic_slice.25
  51.8 4.8 %fusion.55 = f32[1,64,10240]{2,1,0:T(8,128)S(1)} fusion(s32[10240]{0:T(1024)S(1)} %bitcast.90, s32[512]{0:T(512)S(1)} %bitcast.88, f32[1,64,10240]{2,1,0:T(8,128)S(1)} %get-tuple-element.264, pred[]{:T(512)S(6)} %compare.3, bf16[1,64,4096]{2,1,0:T(8,128)(2,1)} %get-tuple-element.275, s32[]{:T(128)S(6)} %select_n.63), kind=kOutput, calls=%fused_computation.5.clone.1 | convolution fusion | flops 677642240 | bytes 5351429 | tf_op jit(solution)/shard_map/while/body/eval_jaxpr/fdr,fre->fde/dot_general | solution.py:35
  56.7 0.1 convert_element_type.41
  56.8 0.2 copy.18
  57.0 0.4 copy-done.1
  57.5 5.2 %fusion.39 = f32[8,1,64,128]{3,2,0,1:T(8,128)} fusion(s32[8,1280]{1,0:T(8,128)S(1)} %bitcast_select_fusion, s32[8,1280]{1,0:T(8,128)S(1)} %bitcast.94, bf16[64,8,1280]{2,1,0:T(8,128)(2,1)S(1)} %bitcast.82), kind=kOutput, calls=%fused_computation.34 | convolution fusion | flops 171704320 | bytes 1654784 | tf_op jit(solution)/shard_map/fdnk,fnkj->nfdj/dot_general | solution.py:50
  62.9 28.1 %all_gather.3 = bf16[1,64,1024]{2,1,0:T(8,128)(2,1)S(1)} all-gather(bf16[1,64,128]{2,1,0:T(8,128)(2,1)S(1)} %copy-done.2), channel_id=1, replica_groups=mesh['rows'=8,'dims'=4] {'rows'}, dimensions={2}, use_global_device_ids=true | all-gather | bytes 147456 | tf_op jit(solution)/shard_map/all_gather | solution.py:55
  91.0 3.1 %fusion.32 = bf16[1,8,8,8,1280]{4,3,2,1,0:T(8,128)(2,1)S(1)} fusion(s32[8,1280]{1,0:T(8,128)S(1)} %bitcast.95, bf16[64,8,128]{2,1,0:T(8,128)(2,1)S(1)} %bitcast.84), kind=kOutput, calls=%fused_computation.27 | convolution fusion | flops 169738240 | bytes 1482752 | tf_op jit(solution)/shard_map/fdnj,fnkj->fdnk/dot_general | solution.py:58
  94.3 38.5 %while.24 = (s32[]{:T(128)}, f32[8,1,64,512]{3,2,1,0:T(8,128)S(1)}, s32[1,1,10240]{2,1,0:T(1,128)S(1)}, s32[8]{0:T(128)S(1)}, bf16[1,1,10240]{2,1,0:T(2,128)(2,1...) while((s32[]{:T(128)}, f32[8,1,64,512]{3,2,1,0:T(8,128)S(1)}, ...), condition=%wide.region_4.5_spmd.clone, body=%wide.region_3.4_spmd.clone.sunk | while | flops 681574912 | bytes 1548423 | solution.py:68
  94.4 0.6 dynamic_slice.23
  95.7 3.4 %fusion.52 = f32[8,1,64,512]{3,2,1,0:T(8,128)S(1)} fusion(f32[8,1,64,512]{3,2,1,0:T(8,128)S(1)} %get-tuple-element.291, s32[]{:T(128)S(6)} %copy.36, bf16[1,64,10240]{2,1,0:T(8,128)(2,1)S(1)} %get-tuple-element.304, s32[10240]{0:T(1024)S(1)} %bitcast.91, s32[512]{0:T(512)S(1)} %bitcast.89, bf16[10240]{0:T(1024)(128)(2,1)S(1)} %reduce.5), kind=kOutput, calls=%fused_computation.20.clone.1 | convolution fusion | flops 681574400 | bytes 1505284 | tf_op jit(solution)/shard_map/while/body/eval_jaxpr/fde,fre->fdr/dot_general | solution.py:66
  99.2 0.6 dynamic_slice.23
  100.5 3.4 %fusion.52 = f32[8,1,64,512]{3,2,1,0:T(8,128)S(1)} fusion(f32[8,1,64,512]{3,2,1,0:T(8,128)S(1)} %get-tuple-element.291, s32[]{:T(128)S(6)} %copy.36, bf16[1,64,10240]{2,1,0:T(8,128)(2,1)S(1)} %get-tuple-element.304, s32[10240]{0:T(1024)S(1)} %bitcast.91, s32[512]{0:T(512)S(1)} %bitcast.89, bf16[10240]{0:T(1024)(128)(2,1)S(1)} %reduce.5), kind=kOutput, calls=%fused_computation.20.clone.1 | convolution fusion | flops 681574400 | bytes 1505284 | tf_op jit(solution)/shard_map/while/body/eval_jaxpr/fde,fre->fdr/dot_general | solution.py:66
  104.0 0.6 dynamic_slice.23
  105.2 0.1 reduce.5
  105.3 3.4 %fusion.52 = f32[8,1,64,512]{3,2,1,0:T(8,128)S(1)} fusion(f32[8,1,64,512]{3,2,1,0:T(8,128)S(1)} %get-tuple-element.291, s32[]{:T(128)S(6)} %copy.36, bf16[1,64,10240]{2,1,0:T(8,128)(2,1)S(1)} %get-tuple-element.304, s32[10240]{0:T(1024)S(1)} %bitcast.91, s32[512]{0:T(512)S(1)} %bitcast.89, bf16[10240]{0:T(1024)(128)(2,1)S(1)} %reduce.5), kind=kOutput, calls=%fused_computation.20.clone.1 | convolution fusion | flops 681574400 | bytes 1505284 | tf_op jit(solution)/shard_map/while/body/eval_jaxpr/fde,fre->fdr/dot_general | solution.py:66
  108.8 0.6 dynamic_slice.23
  110.0 0.1 reduce.5
  110.1 3.4 %fusion.52 = f32[8,1,64,512]{3,2,1,0:T(8,128)S(1)} fusion(f32[8,1,64,512]{3,2,1,0:T(8,128)S(1)} %get-tuple-element.291, s32[]{:T(128)S(6)} %copy.36, bf16[1,64,10240]{2,1,0:T(8,128)(2,1)S(1)} %get-tuple-element.304, s32[10240]{0:T(1024)S(1)} %bitcast.91, s32[512]{0:T(512)S(1)} %bitcast.89, bf16[10240]{0:T(1024)(128)(2,1)S(1)} %reduce.5), kind=kOutput, calls=%fused_computation.20.clone.1 | convolution fusion | flops 681574400 | bytes 1505284 | tf_op jit(solution)/shard_map/while/body/eval_jaxpr/fde,fre->fdr/dot_general | solution.py:66
  113.6 0.6 dynamic_slice.23
  114.8 0.1 reduce.5
  115.0 3.4 %fusion.52 = f32[8,1,64,512]{3,2,1,0:T(8,128)S(1)} fusion(f32[8,1,64,512]{3,2,1,0:T(8,128)S(1)} %get-tuple-element.291, s32[]{:T(128)S(6)} %copy.36, bf16[1,64,10240]{2,1,0:T(8,128)(2,1)S(1)} %get-tuple-element.304, s32[10240]{0:T(1024)S(1)} %bitcast.91, s32[512]{0:T(512)S(1)} %bitcast.89, bf16[10240]{0:T(1024)(128)(2,1)S(1)} %reduce.5), kind=kOutput, calls=%fused_computation.20.clone.1 | convolution fusion | flops 681574400 | bytes 1505284 | tf_op jit(solution)/shard_map/while/body/eval_jaxpr/fde,fre->fdr/dot_general | solution.py:66
  118.4 0.6 dynamic_slice.23
  119.8 3.4 %fusion.52 = f32[8,1,64,512]{3,2,1,0:T(8,128)S(1)} fusion(f32[8,1,64,512]{3,2,1,0:T(8,128)S(1)} %get-tuple-element.291, s32[]{:T(128)S(6)} %copy.36, bf16[1,64,10240]{2,1,0:T(8,128)(2,1)S(1)} %get-tuple-element.304, s32[10240]{0:T(1024)S(1)} %bitcast.91, s32[512]{0:T(512)S(1)} %bitcast.89, bf16[10240]{0:T(1024)(128)(2,1)S(1)} %reduce.5), kind=kOutput, calls=%fused_computation.20.clone.1 | convolution fusion | flops 681574400 | bytes 1505284 | tf_op jit(solution)/shard_map/while/body/eval_jaxpr/fde,fre->fdr/dot_general | solution.py:66
  123.2 0.6 dynamic_slice.23
  124.6 3.4 %fusion.52 = f32[8,1,64,512]{3,2,1,0:T(8,128)S(1)} fusion(f32[8,1,64,512]{3,2,1,0:T(8,128)S(1)} %get-tuple-element.291, s32[]{:T(128)S(6)} %copy.36, bf16[1,64,10240]{2,1,0:T(8,128)(2,1)S(1)} %get-tuple-element.304, s32[10240]{0:T(1024)S(1)} %bitcast.91, s32[512]{0:T(512)S(1)} %bitcast.89, bf16[10240]{0:T(1024)(128)(2,1)S(1)} %reduce.5), kind=kOutput, calls=%fused_computation.20.clone.1 | convolution fusion | flops 681574400 | bytes 1505284 | tf_op jit(solution)/shard_map/while/body/eval_jaxpr/fde,fre->fdr/dot_general | solution.py:66
  128.0 0.6 dynamic_slice.23
  129.4 3.4 %fusion.52 = f32[8,1,64,512]{3,2,1,0:T(8,128)S(1)} fusion(f32[8,1,64,512]{3,2,1,0:T(8,128)S(1)} %get-tuple-element.291, s32[]{:T(128)S(6)} %copy.36, bf16[1,64,10240]{2,1,0:T(8,128)(2,1)S(1)} %get-tuple-element.304, s32[10240]{0:T(1024)S(1)} %bitcast.91, s32[512]{0:T(512)S(1)} %bitcast.89, bf16[10240]{0:T(1024)(128)(2,1)S(1)} %reduce.5), kind=kOutput, calls=%fused_computation.20.clone.1 | convolution fusion | flops 681574400 | bytes 1505284 | tf_op jit(solution)/shard_map/while/body/eval_jaxpr/fde,fre->fdr/dot_general | solution.py:66
  132.8 0.2 multiply_reduce_fusion
  133.1 10.1 %psum.7 = f32[1,4096]{1,0:T(1,128)S(1)} all-reduce(f32[1,4096]{1,0:T(1,128)S(1)} %bitcast.87), channel_id=1, replica_groups=mesh['rows'=8,'dims'=4] {'dims'}, use_global_device_ids=true, to_apply=%region_6.7 | all-reduce | flops 4096 | bytes 32768 | tf_op jit(solution)/shard_map/psum | solution.py:71
  143.2 0.6 fusion.45
  143.9 0.9 subtract_convert_fusion
  (50 shorter events, 1.3 us)
Async XLA Ops:
  7.2 137.7 %reduce-scatter.2.cloned.1.call-start = ((), (), s32[]{:S(2)}) async-start(), calls=%async_computation.1 | async-start | bytes 294912 | tf_op jit(solution)/shard_map/reduce_scatter | solution.py:49
  56.6 0.8 copy-start.1
  56.6 0.8 copy-start.4
  56.7 0.8 copy-start.5
  57.5 5.4 %copy-start.2 = (bf16[1,64,128]{2,1,0:T(8,128)(2,1)S(1)}, bf16[1,64,128]{2,1,0:T(8,128)(2,1)}, u32[]{:S(2)}) copy-start(bf16[1,64,128]{2,1,0:T(8,128)(2,1)} %param.13) | copy-start | bytes 49156
  132.8 10.4 %copy-start.3 = (f32[1,4096]{1,0:T(1,128)S(1)}, f32[1,4096]{1,0:T(1,128)}, u32[]{:S(2)}) copy-start(f32[1,4096]{1,0:T(1,128)} %param.12) | copy-start | bytes 49156
  132.8 11.1 %copy-start = (bf16[1,64,4096]{2,1,0:T(8,128)(2,1)S(1)}, bf16[1,64,4096]{2,1,0:T(8,128)(2,1)}, u32[]{:S(2)}) copy-start(bf16[1,64,4096]{2,1,0:T(8,128)(2,1)} %get-tuple-element.309) | copy-start | bytes 1572868
Sparse Core Ops, SparseCore 0:
  62.8 64.8 reduce-scatter.1
where the time goes:
time: 152 us
  matrix products  73.9 us (49%)
  blocking collectives  38.2 us (25%)
  between operations  14.2 us (9%)
  local copies, waits for them, and re-layouts  11.3 us (7%)
  loops' own time  11 us (7%)
  other arithmetic  3.03 us (2%)
    dot_general x8, matrix products, lookup_block(): jnp.einsum('fdr,fre->fde', table_part, selector, preferred_element_type=j...  38.3 us
    all_gather x1, blocking collectives, shards(): all_grads = lax.all_gather(grad_pooled, 'rows', axis=2, tiled=True)  28.1 us
    dot_general x8, matrix products, gradient_block(): jnp.einsum('fde,fre->fdr', entry_flat, weighted, preferred_element_type=j...  27.4 us
    psum x1, blocking collectives, shards(): norm_total = lax.psum(squares, 'dims')  10.1 us
    dynamic_slice x16, local copies, waits for them, and re-layouts, shards(): lax.scan(lookup_block, jnp.zeros((feat_count, dim_local, entry_count), jn...  9.38 us
    another operation x1, loops' own time, shards(): lax.scan(lookup_block, jnp.zeros((feat_count, dim_local, entry_count), jn...  5.55 us
    another operation x1, loops' own time, shards(): lax.map(gradient_block, jnp.arange(block_count, dtype=jnp.int32))  5.46 us
    dot_general x1, matrix products, shards(): jnp.einsum('fdnk,fnkj->nfdj', picked, onehot, preferred_element_type=jnp....  5.15 us
  transfers between devices with their start and end apart: 1, of which 0 were waited for; matrix products, arithmetic and copies ran while one was open for 25% of the time, Pallas kernels for 0%

commit v1 on v0

--- a/solution.py
+++ b/solution.py
@@ -6,6 +6,14 @@
 
 D = 256
 step_size = 0.3
+
+
+def sum_by_hops(x, axis):
+    peers, result = (lax.axis_size(axis), x)
+    for far in [1 << k for k in range(peers.bit_length() - 1)]:
+        swap = [(i, i ^ far) for i in range(peers)]
+        result = result + lax.ppermute(result, axis, swap)
+    return result
 
 
 def shards(table, accum, grad_pooled, sample_slot, row_slot, weight, send_count):
@@ -68,7 +76,7 @@
     grad_blocks = lax.map(gradient_block, jnp.arange(block_count, dtype=jnp.int32))
     row_grad = jnp.moveaxis(grad_blocks, 0, 2).reshape(feat_count, dim_local, row_local)
     squares = jnp.sum(row_grad * row_grad, axis=1)
-    norm_total = lax.psum(squares, "dims")
+    norm_total = sum_by_hops(squares, "dims")
     new_accum = accum + norm_total / D
     new_table = (
         table.astype(jnp.float32) - step_size * row_grad / jnp.sqrt(new_accum)[:, None, :]

time: 152 us -> 223 us (1.47)
  waiting for transfers between devices: 0.02 us -> 58.9 us
  matrix products: 73.9 us -> 91.5 us
  blocking collectives: 38.2 us -> 28.2 us
    reduce_scatter x1, waiting for transfers between devices: 0.01 us -> 58.9 us  [shards(): lax.psum_scatter(jnp.einsum('fdnk,fnkj->nfdj', picked, onehot, preferred_...]
    dot_general x8, matrix products: 38.3 us -> 55.1 us  [lookup_block(): jnp.einsum('fdr,fre->fde', table_part, selector, preferred_element_type=j...]
    psum x1 -> x0, blocking collectives: 10.1 us -> none  [shards(): norm_total = lax.psum(squares, 'dims')]
  transfers between devices with their start and end apart: 1 -> 3, of which waited for: 0 -> 1; matrix products, arithmetic and copies ran while one was open for 25% -> 31% of each run, Pallas kernels for 0% -> 0%
where the time goes in v1:
time: 223 us; the launch traced here: 222 us
  matrix products  91.5 us (41%)
  waiting for transfers between devices  58.9 us (26%)
  blocking collectives  28.2 us (13%)
  between operations  14.2 us (6%)
  local copies, waits for them, and re-layouts  12.3 us (6%)
  loops' own time  10.8 us (5%)
  other arithmetic  4.81 us (2%)
    reduce_scatter x1, waiting for transfers between devices, shards(): lax.psum_scatter(jnp.einsum('fdnk,fnkj->nfdj', picked, onehot, preferred_...  58.9 us
    dot_general x8, matrix products, lookup_block(): jnp.einsum('fdr,fre->fde', table_part, selector, preferred_element_type=j...  55.1 us
    all_gather x1, blocking collectives, shards(): all_grads = lax.all_gather(grad_pooled, 'rows', axis=2, tiled=True)  28.2 us
    dot_general x8, matrix products, gradient_block(): jnp.einsum('fde,fre->fdr', entry_flat, weighted, preferred_element_type=j...  27.3 us
    dynamic_slice x16, local copies, waits for them, and re-layouts, shards(): lax.scan(lookup_block, jnp.zeros((feat_count, dim_local, entry_count), jn...  9.35 us
    another operation x1, loops' own time, shards(): lax.map(gradient_block, jnp.arange(block_count, dtype=jnp.int32))  5.46 us
    another operation x1, loops' own time, shards(): lax.scan(lookup_block, jnp.zeros((feat_count, dim_local, entry_count), jn...  5.39 us
    dot_general x1, matrix products, shards(): jnp.einsum('fdnk,fnkj->nfdj', picked, onehot, preferred_element_type=jnp....  5.15 us
  transfers between devices with their start and end apart: 3, of which 1 were waited for; matrix products, arithmetic and copies ran while one was open for 31% of the time, Pallas kernels for 0%

profile of v1, /device:TPU:0, one launch (start us, length us, event | category | flops | bytes accessed | tf_op | source)
XLA Modules:
  0.0 222.4 jit_solution(11633399811877562371)
XLA Ops:
  7.2 0.8 reshape_reshape.3
  8.0 0.8 reshape.272
  8.9 0.7 lt.56
  9.7 28.2 %all_gather.3 = bf16[1,64,1024]{2,1,0:T(8,128)(2,1)S(1)} all-gather(bf16[1,64,128]{2,1,0:T(8,128)(2,1)} %param.13), channel_id=1, replica_groups=mesh['rows'=8,'dims'=4] {'rows'}, dimensions={2}, use_global_device_ids=true | all-gather | bytes 147456 | tf_op jit(solution)/shard_map/all_gather | solution.py:63
  37.9 3.9 %fusion.32 = bf16[1,8,8,8,1280]{4,3,2,1,0:T(8,128)(2,1)S(1)} fusion(s32[8,1280]{1,0:T(8,128)} %bitcast.95, bf16[64,8,128]{2,1,0:T(8,128)(2,1)S(1)} %bitcast.84), kind=kOutput, calls=%fused_computation.27 | convolution fusion | flops 169738240 | bytes 1482752 | tf_op jit(solution)/shard_map/fdnj,fnkj->fdnk/dot_general | solution.py:66
  42.0 38.4 %while.24 = (s32[]{:T(128)}, f32[8,1,64,512]{3,2,1,0:T(8,128)S(1)}, s32[1,1,10240]{2,1,0:T(1,128)S(1)}, s32[8]{0:T(128)S(1)}, bf16[1,1,10240]{2,1,0:T(2,128)(2,1...) while((s32[]{:T(128)}, f32[8,1,64,512]{3,2,1,0:T(8,128)S(1)}, ...), condition=%wide.region_4.5_spmd.clone, body=%wide.region_3.4_spmd.clone.sunk | while | flops 681574912 | bytes 1548423 | solution.py:76
  42.0 0.6 dynamic_slice.23
  43.3 0.1 reduce.5
  43.4 3.4 %fusion.52 = f32[8,1,64,512]{3,2,1,0:T(8,128)S(1)} fusion(f32[8,1,64,512]{3,2,1,0:T(8,128)S(1)} %get-tuple-element.291, s32[]{:T(128)S(6)} %copy.36, bf16[1,64,10240]{2,1,0:T(8,128)(2,1)S(1)} %get-tuple-element.304, s32[10240]{0:T(1024)S(1)} %bitcast.91, s32[512]{0:T(512)S(1)} %bitcast.90, bf16[10240]{0:T(1024)(128)(2,1)S(1)} %reduce.5), kind=kOutput, calls=%fused_computation.20.clone.1 | convolution fusion | flops 681574400 | bytes 1505284 | tf_op jit(solution)/shard_map/while/body/eval_jaxpr/fde,fre->fdr/dot_general | solution.py:74
  46.8 0.6 dynamic_slice.23
  48.2 3.4 %fusion.52 = f32[8,1,64,512]{3,2,1,0:T(8,128)S(1)} fusion(f32[8,1,64,512]{3,2,1,0:T(8,128)S(1)} %get-tuple-element.291, s32[]{:T(128)S(6)} %copy.36, bf16[1,64,10240]{2,1,0:T(8,128)(2,1)S(1)} %get-tuple-element.304, s32[10240]{0:T(1024)S(1)} %bitcast.91, s32[512]{0:T(512)S(1)} %bitcast.90, bf16[10240]{0:T(1024)(128)(2,1)S(1)} %reduce.5), kind=kOutput, calls=%fused_computation.20.clone.1 | convolution fusion | flops 681574400 | bytes 1505284 | tf_op jit(solution)/shard_map/while/body/eval_jaxpr/fde,fre->fdr/dot_general | solution.py:74
  51.6 0.6 dynamic_slice.23
  53.0 3.4 %fusion.52 = f32[8,1,64,512]{3,2,1,0:T(8,128)S(1)} fusion(f32[8,1,64,512]{3,2,1,0:T(8,128)S(1)} %get-tuple-element.291, s32[]{:T(128)S(6)} %copy.36, bf16[1,64,10240]{2,1,0:T(8,128)(2,1)S(1)} %get-tuple-element.304, s32[10240]{0:T(1024)S(1)} %bitcast.91, s32[512]{0:T(512)S(1)} %bitcast.90, bf16[10240]{0:T(1024)(128)(2,1)S(1)} %reduce.5), kind=kOutput, calls=%fused_computation.20.clone.1 | convolution fusion | flops 681574400 | bytes 1505284 | tf_op jit(solution)/shard_map/while/body/eval_jaxpr/fde,fre->fdr/dot_general | solution.py:74
  56.4 0.6 dynamic_slice.23
  57.8 3.4 %fusion.52 = f32[8,1,64,512]{3,2,1,0:T(8,128)S(1)} fusion(f32[8,1,64,512]{3,2,1,0:T(8,128)S(1)} %get-tuple-element.291, s32[]{:T(128)S(6)} %copy.36, bf16[1,64,10240]{2,1,0:T(8,128)(2,1)S(1)} %get-tuple-element.304, s32[10240]{0:T(1024)S(1)} %bitcast.91, s32[512]{0:T(512)S(1)} %bitcast.90, bf16[10240]{0:T(1024)(128)(2,1)S(1)} %reduce.5), kind=kOutput, calls=%fused_computation.20.clone.1 | convolution fusion | flops 681574400 | bytes 1505284 | tf_op jit(solution)/shard_map/while/body/eval_jaxpr/fde,fre->fdr/dot_general | solution.py:74
  61.2 0.6 dynamic_slice.23
  62.6 3.4 %fusion.52 = f32[8,1,64,512]{3,2,1,0:T(8,128)S(1)} fusion(f32[8,1,64,512]{3,2,1,0:T(8,128)S(1)} %get-tuple-element.291, s32[]{:T(128)S(6)} %copy.36, bf16[1,64,10240]{2,1,0:T(8,128)(2,1)S(1)} %get-tuple-element.304, s32[10240]{0:T(1024)S(1)} %bitcast.91, s32[512]{0:T(512)S(1)} %bitcast.90, bf16[10240]{0:T(1024)(128)(2,1)S(1)} %reduce.5), kind=kOutput, calls=%fused_computation.20.clone.1 | convolution fusion | flops 681574400 | bytes 1505284 | tf_op jit(solution)/shard_map/while/body/eval_jaxpr/fde,fre->fdr/dot_general | solution.py:74
  66.0 0.6 dynamic_slice.23
  67.4 3.4 %fusion.52 = f32[8,1,64,512]{3,2,1,0:T(8,128)S(1)} fusion(f32[8,1,64,512]{3,2,1,0:T(8,128)S(1)} %get-tuple-element.291, s32[]{:T(128)S(6)} %copy.36, bf16[1,64,10240]{2,1,0:T(8,128)(2,1)S(1)} %get-tuple-element.304, s32[10240]{0:T(1024)S(1)} %bitcast.91, s32[512]{0:T(512)S(1)} %bitcast.90, bf16[10240]{0:T(1024)(128)(2,1)S(1)} %reduce.5), kind=kOutput, calls=%fused_computation.20.clone.1 | convolution fusion | flops 681574400 | bytes 1505284 | tf_op jit(solution)/shard_map/while/body/eval_jaxpr/fde,fre->fdr/dot_general | solution.py:74
  70.8 0.6 dynamic_slice.23
  72.2 3.4 %fusion.52 = f32[8,1,64,512]{3,2,1,0:T(8,128)S(1)} fusion(f32[8,1,64,512]{3,2,1,0:T(8,128)S(1)} %get-tuple-element.291, s32[]{:T(128)S(6)} %copy.36, bf16[1,64,10240]{2,1,0:T(8,128)(2,1)S(1)} %get-tuple-element.304, s32[10240]{0:T(1024)S(1)} %bitcast.91, s32[512]{0:T(512)S(1)} %bitcast.90, bf16[10240]{0:T(1024)(128)(2,1)S(1)} %reduce.5), kind=kOutput, calls=%fused_computation.20.clone.1 | convolution fusion | flops 681574400 | bytes 1505284 | tf_op jit(solution)/shard_map/while/body/eval_jaxpr/fde,fre->fdr/dot_general | solution.py:74
  75.6 0.6 dynamic_slice.23
  77.0 3.4 %fusion.52 = f32[8,1,64,512]{3,2,1,0:T(8,128)S(1)} fusion(f32[8,1,64,512]{3,2,1,0:T(8,128)S(1)} %get-tuple-element.291, s32[]{:T(128)S(6)} %copy.36, bf16[1,64,10240]{2,1,0:T(8,128)(2,1)S(1)} %get-tuple-element.304, s32[10240]{0:T(1024)S(1)} %bitcast.91, s32[512]{0:T(512)S(1)} %bitcast.90, bf16[10240]{0:T(1024)(128)(2,1)S(1)} %reduce.5), kind=kOutput, calls=%fused_computation.20.clone.1 | convolution fusion | flops 681574400 | bytes 1505284 | tf_op jit(solution)/shard_map/while/body/eval_jaxpr/fde,fre->fdr/dot_general | solution.py:74
  80.4 0.2 multiply_reduce_fusion
  80.8 65.2 %while.25 = (s32[]{:T(128)}, f32[1,64,10240]{2,1,0:T(8,128)}, s32[8]{0:T(128)S(1)}, bf16[1,64,4096]{2,1,0:T(8,128)(2,1)S(1)}, s32[1,1,10240]{2,1,0:T(1,128)S(1)}...) while((s32[]{:T(128)}, f32[1,64,10240]{2,1,0:T(8,128)}, s32[8]{0:T(128)S(1)}, ...), condition=%wide.region_1.2_spmd.clone, body=%wide.region_0.1_spmd.clone.sunk | while | flops 677642752 | bytes 5353649 | solution.py:47
  80.8 0.6 dynamic_slice.25
  82.0 5.4 %fusion.55 = f32[1,64,10240]{2,1,0:T(8,128)} fusion(s32[10240]{0:T(1024)S(1)} %bitcast.92, s32[512]{0:T(512)S(1)} %bitcast.89, f32[1,64,10240]{2,1,0:T(8,128)} %get-tuple-element.264, pred[]{:T(512)S(6)} %compare.3, bf16[1,64,4096]{2,1,0:T(8,128)(2,1)S(1)} %get-tuple-element.275, s32[]{:T(128)S(6)} %select_n.63), kind=kOutput, calls=%fused_computation.5.clone.1 | convolution fusion | flops 677642240 | bytes 5351429 | tf_op jit(solution)/shard_map/while/body/eval_jaxpr/fdr,fre->fde/dot_general | solution.py:43
  87.4 0.6 dynamic_slice.25
  88.7 7.1 %fusion.55 = f32[1,64,10240]{2,1,0:T(8,128)} fusion(s32[10240]{0:T(1024)S(1)} %bitcast.92, s32[512]{0:T(512)S(1)} %bitcast.89, f32[1,64,10240]{2,1,0:T(8,128)} %get-tuple-element.264, pred[]{:T(512)S(6)} %compare.3, bf16[1,64,4096]{2,1,0:T(8,128)(2,1)S(1)} %get-tuple-element.275, s32[]{:T(128)S(6)} %select_n.63), kind=kOutput, calls=%fused_computation.5.clone.1 | convolution fusion | flops 677642240 | bytes 5351429 | tf_op jit(solution)/shard_map/while/body/eval_jaxpr/fdr,fre->fde/dot_general | solution.py:43
  95.8 0.6 dynamic_slice.25
  97.0 7.1 %fusion.55 = f32[1,64,10240]{2,1,0:T(8,128)} fusion(s32[10240]{0:T(1024)S(1)} %bitcast.92, s32[512]{0:T(512)S(1)} %bitcast.89, f32[1,64,10240]{2,1,0:T(8,128)} %get-tuple-element.264, pred[]{:T(512)S(6)} %compare.3, bf16[1,64,4096]{2,1,0:T(8,128)(2,1)S(1)} %get-tuple-element.275, s32[]{:T(128)S(6)} %select_n.63), kind=kOutput, calls=%fused_computation.5.clone.1 | convolution fusion | flops 677642240 | bytes 5351429 | tf_op jit(solution)/shard_map/while/body/eval_jaxpr/fdr,fre->fde/dot_general | solution.py:43
  104.1 0.6 dynamic_slice.25
  105.4 7.1 %fusion.55 = f32[1,64,10240]{2,1,0:T(8,128)} fusion(s32[10240]{0:T(1024)S(1)} %bitcast.92, s32[512]{0:T(512)S(1)} %bitcast.89, f32[1,64,10240]{2,1,0:T(8,128)} %get-tuple-element.264, pred[]{:T(512)S(6)} %compare.3, bf16[1,64,4096]{2,1,0:T(8,128)(2,1)S(1)} %get-tuple-element.275, s32[]{:T(128)S(6)} %select_n.63), kind=kOutput, calls=%fused_computation.5.clone.1 | convolution fusion | flops 677642240 | bytes 5351429 | tf_op jit(solution)/shard_map/while/body/eval_jaxpr/fdr,fre->fde/dot_general | solution.py:43
  112.5 0.6 dynamic_slice.25
  113.8 7.1 %fusion.55 = f32[1,64,10240]{2,1,0:T(8,128)} fusion(s32[10240]{0:T(1024)S(1)} %bitcast.92, s32[512]{0:T(512)S(1)} %bitcast.89, f32[1,64,10240]{2,1,0:T(8,128)} %get-tuple-element.264, pred[]{:T(512)S(6)} %compare.3, bf16[1,64,4096]{2,1,0:T(8,128)(2,1)S(1)} %get-tuple-element.275, s32[]{:T(128)S(6)} %select_n.63), kind=kOutput, calls=%fused_computation.5.clone.1 | convolution fusion | flops 677642240 | bytes 5351429 | tf_op jit(solution)/shard_map/while/body/eval_jaxpr/fdr,fre->fde/dot_general | solution.py:43
  120.9 0.6 dynamic_slice.25
  122.1 7.1 %fusion.55 = f32[1,64,10240]{2,1,0:T(8,128)} fusion(s32[10240]{0:T(1024)S(1)} %bitcast.92, s32[512]{0:T(512)S(1)} %bitcast.89, f32[1,64,10240]{2,1,0:T(8,128)} %get-tuple-element.264, pred[]{:T(512)S(6)} %compare.3, bf16[1,64,4096]{2,1,0:T(8,128)(2,1)S(1)} %get-tuple-element.275, s32[]{:T(128)S(6)} %select_n.63), kind=kOutput, calls=%fused_computation.5.clone.1 | convolution fusion | flops 677642240 | bytes 5351429 | tf_op jit(solution)/shard_map/while/body/eval_jaxpr/fdr,fre->fde/dot_general | solution.py:43
  129.2 0.6 dynamic_slice.25
  130.5 7.1 %fusion.55 = f32[1,64,10240]{2,1,0:T(8,128)} fusion(s32[10240]{0:T(1024)S(1)} %bitcast.92, s32[512]{0:T(512)S(1)} %bitcast.89, f32[1,64,10240]{2,1,0:T(8,128)} %get-tuple-element.264, pred[]{:T(512)S(6)} %compare.3, bf16[1,64,4096]{2,1,0:T(8,128)(2,1)S(1)} %get-tuple-element.275, s32[]{:T(128)S(6)} %select_n.63), kind=kOutput, calls=%fused_computation.5.clone.1 | convolution fusion | flops 677642240 | bytes 5351429 | tf_op jit(solution)/shard_map/while/body/eval_jaxpr/fdr,fre->fde/dot_general | solution.py:43
  137.6 0.6 dynamic_slice.25
  138.8 7.1 %fusion.55 = f32[1,64,10240]{2,1,0:T(8,128)} fusion(s32[10240]{0:T(1024)S(1)} %bitcast.92, s32[512]{0:T(512)S(1)} %bitcast.89, f32[1,64,10240]{2,1,0:T(8,128)} %get-tuple-element.264, pred[]{:T(512)S(6)} %compare.3, bf16[1,64,4096]{2,1,0:T(8,128)(2,1)S(1)} %get-tuple-element.275, s32[]{:T(128)S(6)} %select_n.63), kind=kOutput, calls=%fused_computation.5.clone.1 | convolution fusion | flops 677642240 | bytes 5351429 | tf_op jit(solution)/shard_map/while/body/eval_jaxpr/fdr,fre->fde/dot_general | solution.py:43
  146.0 1.9 convert_element_type.41
  147.9 0.2 copy.18
  148.2 1.6 collective-permute-start.1
  149.7 5.1 %fusion.39 = f32[8,1,64,128]{3,2,0,1:T(8,128)} fusion(s32[8,1280]{1,0:T(8,128)S(1)} %bitcast_select_fusion, s32[8,1280]{1,0:T(8,128)S(1)} %bitcast.96, bf16[64,8,1280]{2,1,0:T(8,128)(2,1)S(1)} %bitcast.82), kind=kOutput, calls=%fused_computation.34 | convolution fusion | flops 171704320 | bytes 1654784 | tf_op jit(solution)/shard_map/fdnk,fnkj->nfdj/dot_general | solution.py:58
  155.0 0.6 fusion.45
  155.7 0.9 subtract_convert_fusion
  156.6 58.9 %reduce-scatter.2.cloned.1.call-done = f32[1,1,64,128]{3,2,0,1:T(8,128)} async-done(((f32[8,1,64,128]{3,2,0,1:T(8,128)}), f32[1,1,64,128]{3,2,0,1:T(8,128)}) %reduce-scatter.2.cloned.1.call-update) | async-done | bytes 32784 | tf_op jit(solution)/shard_map/reduce_scatter | solution.py:57
  (52 shorter events, 1.5 us)
Async XLA Ops:
  7.2 208.4 %reduce-scatter.2.cloned.1.call-start = ((), (), s32[]{:S(2)}) async-start(), calls=%async_computation.1 | async-start | bytes 294912 | tf_op jit(solution)/shard_map/reduce_scatter | solution.py:57
  42.0 38.8 %copy-start = (bf16[1,64,4096]{2,1,0:T(8,128)(2,1)S(1)}, bf16[1,64,4096]{2,1,0:T(8,128)(2,1)}, u32[]{:S(2)}) copy-start(bf16[1,64,4096]{2,1,0:T(8,128)(2,1)} %param.11) | copy-start | bytes 1572868
  80.6 67.5 %collective-permute-start = (f32[1,4096]{1,0:T(1,128)S(1)}, f32[1,4096]{1,0:T(1,128)S(1)}, u32[]{:S(2)}, u32[]{:S(2)}) collective-permute-start(f32[1,4096]{1,0:T(1,128)S(1)} %bitcast.87), channel_id=1, source_target_pairs={{0,1},{1,0},{2,3},{3,2},{4,5},{5,4},{6,7},{7,6},{8,9},{9,8},{10,11... | collective-permute-start | bytes 49160 | tf_op jit(solution)/shard_map/ppermute | solution.py:15
  80.7 65.2 %copy-start.1 = (s32[1,1,8,1280]{3,2,1,0:T(8,128)S(1)}, s32[1,1,8,1280]{3,2,1,0:T(8,128)}, u32[]{:S(2)}) copy-start(s32[1,1,8,1280]{3,2,1,0:T(8,128)} %param.16) | copy-start | bytes 122884
  80.8 65.2 %copy-start.3 = (s32[1,1,8]{2,1,0:T(1,128)S(1)}, s32[1,1,8]{2,1,0:T(1,128)}, u32[]{:S(2)}) copy-start(s32[1,1,8]{2,1,0:T(1,128)} %param.17) | copy-start | bytes 100
  146.0 3.7 %copy-start.4 = (s32[1,1,8,1280]{3,2,1,0:T(8,128)S(1)}, s32[1,1,8,1280]{3,2,1,0:T(8,128)}, u32[]{:S(2)}) copy-start(s32[1,1,8,1280]{3,2,1,0:T(8,128)} %param.14) | copy-start | bytes 122884
  148.2 6.8 %collective-permute-start.1 = (f32[1,4096]{1,0:T(1,128)S(1)}, f32[1,4096]{1,0:T(1,128)S(1)}, u32[]{:S(2)}, u32[]{:S(2)}) collective-permute-start(f32[1,4096]{1,0:T(1,128)S(1)} %add.57), channel_id=1, source_target_pairs={{0,2},{1,3},{2,0},{3,1},{4,6},{5,7},{6,4},{7,5},{8,10},{9,11},{10,... | collective-permute-start | bytes 49160 | tf_op jit(solution)/shard_map/ppermute | solution.py:15
  149.7 5.3 %copy-start.2 = (f32[1,4096]{1,0:T(1,128)S(1)}, f32[1,4096]{1,0:T(1,128)}, u32[]{:S(2)}) copy-start(f32[1,4096]{1,0:T(1,128)} %param.12) | copy-start | bytes 49156
Sparse Core Ops, SparseCore 0:
  155.0 60.4 reduce-scatter.1
